TPU v7x, 128 devices: a whole 4x4x4 slice. The times are simulated.
128 devices in a mesh: mesh: 16 (over z, x), bg: 8 (over y, core).
Axes of the slice: x: 4, y: 4, z: 4, core: 2. Of those that a mesh axis runs over, the one named last changes fastest.
Arguments:
- displacement: float32 [3, 64, 32, 128], P(None, 'mesh', 'bg'), may hold values from -0.4 to 0.4
- bg_coef: float32 [8, 2097152], P(None, ('mesh', 'bg')), may hold values from -0.3 to 0.3
- query_elem: int32 [128, 128, 136], P(('mesh', 'bg')), may hold values from 0 to 16383
- query_point: int32 [128, 128, 136], P(('mesh', 'bg')), may hold values from 0 to 6912, as said below
- query_coord: float32 [128, 128, 3, 136], P(('mesh', 'bg')), may hold values from 0 to 1
Outputs:
- new_displacement: float32 [3, 64, 32, 128], P(None, 'mesh', 'bg')
- line_coeffs: float32 [2, 5], replicated
Inputs may be any that keep to these rules, and one draw needn't show every extreme that they name: `query_point`: in each row every quadrature point 0 to 6911 of the row's device fills exactly one slot; all other slots hold 6912 and are empty. In every draw some owner's bucket is full in every row.
All inputs are finite; a program needn't handle non-finite values.
Results may differ from a plain program's by a relative error of at most 0.0003.
Values sent between devices are 32-bit elements; how exact they have to be, the bound alone decides.
No kernel may reach another device: no remote copies, remote signals or barrier semaphores. Data moves between devices by JAX's collectives and lax.ppermute only.
A program may use at most 64 MiB of HBM per device.

v0:
```python
import jax
import jax.numpy as jnp
import numpy as np
from jax import lax
from jax.sharding import PartitionSpec as P

PASSES = 2
LS_STEPS = 4
GAUSS_POINTS = np.array([0.5 - 0.5 * np.sqrt(0.6), 0.5, 0.5 + 0.5 * np.sqrt(0.6)])
GAUSS_WEIGHTS = np.array([5.0 / 18.0, 8.0 / 18.0, 5.0 / 18.0])


def extended(block, sides, width):
    for axis, dim in sides:
        count = lax.axis_size(axis)
        forward = [(i, i + 1) for i in range(count - 1)]
        forward.append((count - 1, 0))
        backward = [(target, source) for source, target in forward]
        low = lax.ppermute(
            lax.slice_in_dim(block, block.shape[dim] - width, None, axis=dim), axis, forward
        )
        high = lax.ppermute(lax.slice_in_dim(block, 0, width, axis=dim), axis, backward)
        block = jnp.concatenate([low, block, high], axis=dim)
    return block


def basis_tables(elements, periodic):
    node_count = 2 * elements if periodic else 2 * elements + 1
    values = np.zeros((node_count, 3 * elements))
    slopes = np.zeros((node_count, 3 * elements))
    points = GAUSS_POINTS
    shape_values = [
        2.0 * (points - 0.5) * (points - 1.0),
        -4.0 * points * (points - 1.0),
        2.0 * points * (points - 0.5),
    ]
    shape_slopes = [4.0 * points - 3.0, 4.0 - 8.0 * points, 4.0 * points - 1.0]
    for offset in range(3):
        node_rows = (2 * np.arange(elements) + offset) % node_count
        for gauss_index in range(3):
            columns = 3 * np.arange(elements) + gauss_index
            values[node_rows, columns] += shape_values[offset][gauss_index]
            slopes[node_rows, columns] += shape_slopes[offset][gauss_index]
    return (jnp.asarray(values, dtype=jnp.float32), jnp.asarray(slopes, dtype=jnp.float32))


def quad_weights(z_elems, y_elems, x_elems):
    along_z = jnp.asarray(np.tile(GAUSS_WEIGHTS, z_elems), dtype=jnp.float32)
    along_y = jnp.asarray(np.tile(GAUSS_WEIGHTS, y_elems), dtype=jnp.float32)
    along_x = jnp.asarray(np.tile(GAUSS_WEIGHTS, x_elems), dtype=jnp.float32)
    return along_z[:, None, None] * along_y[None, :, None] * along_x[None, None, :]


def gradients(node_field, tables):
    z_value, z_slope, y_value, y_slope, value_along_x, x_slope = tables
    highest = lax.Precision.HIGHEST
    value_z = jnp.einsum("czyx,zk->ckyx", node_field, z_value, precision=highest)
    slope_z = jnp.einsum("czyx,zk->ckyx", node_field, z_slope, precision=highest)
    value_zy = jnp.einsum("ckyx,yl->cklx", value_z, y_value, precision=highest)
    slope_y = jnp.einsum("ckyx,yl->cklx", value_z, y_slope, precision=highest)
    slope_zy = jnp.einsum("ckyx,yl->cklx", slope_z, y_value, precision=highest)
    deriv_x = jnp.einsum("cklx,xm->cklm", value_zy, x_slope, precision=highest)
    deriv_y = jnp.einsum("cklx,xm->cklm", slope_y, value_along_x, precision=highest)
    deriv_z = jnp.einsum("cklx,xm->cklm", slope_zy, value_along_x, precision=highest)
    return jnp.stack([deriv_x, deriv_y, deriv_z], axis=1)


def identity_block():
    return jnp.eye(3, dtype=jnp.float32)[:, :, None, None, None]


def gram(left_part, right_part):
    return jnp.sum(left_part[:, :, None] * right_part[:, None, :], axis=0)


def energy(node_field, tables, target_size_scale, weights):
    jacobian = gradients(node_field, tables) + identity_block()
    strain = gram(jacobian, jacobian) * target_size_scale - identity_block()
    return jnp.sum(weights * jnp.sum(strain * strain, axis=(0, 1)))


def line_terms(node_field, direction, tables, target_size_scale, weights):
    jacobian = gradients(node_field, tables) + identity_block()
    motion = gradients(direction, tables)
    strain_zero = gram(jacobian, jacobian) * target_size_scale - identity_block()
    mixed = gram(jacobian, motion)
    strain_one = (mixed + jnp.swapaxes(mixed, 0, 1)) * target_size_scale
    strain_two = gram(motion, motion) * target_size_scale

    def weighted(first_part, latter_portion):
        return jnp.sum(weights * jnp.sum(first_part * latter_portion, axis=(0, 1)))

    zero_zero = weighted(strain_zero, strain_zero)
    zero_one = weighted(strain_zero, strain_one)
    zero_two = weighted(strain_zero, strain_two)
    one_two = weighted(strain_one, strain_two)
    two_two = weighted(strain_two, strain_two)
    gauss_newton = weighted(strain_one, strain_one)
    return (
        zero_zero,
        2.0 * zero_one,
        gauss_newton + 2.0 * zero_two,
        2.0 * one_two,
        two_two,
        gauss_newton,
    )


def line_search(terms):
    const_term, linear, quadratic, cubic_term, quartic, gauss_newton = terms
    step_len = jnp.zeros((), jnp.float32)
    for search_turn in range(LS_STEPS):
        slope = linear + step_len * (
            2.0 * quadratic + step_len * (3.0 * cubic_term + step_len * 4.0 * quartic)
        )
        curvature = 2.0 * quadratic + step_len * (6.0 * cubic_term + step_len * 12.0 * quartic)
        step_len = step_len - slope / jnp.maximum(curvature, gauss_newton + 1e-06)
    return step_len


def inverse_square(coefs, coords):
    along_x = coords[:, 0]
    along_y = coords[:, 1]
    along_z = coords[:, 2]
    summed = jnp.zeros_like(along_x)
    for corner in range(8):
        weight_x = along_x if corner & 1 else 1.0 - along_x
        weight_y = along_y if corner & 2 else 1.0 - along_y
        weight_z = along_z if corner & 4 else 1.0 - along_z
        summed = summed + weight_x * weight_y * weight_z * coefs[:, corner]
    return jnp.exp(-2.0 * summed)


def gather_coefs(table, elem_ids):
    index_rows = elem_ids[:, 0, :]
    corner_rows = jnp.take(jnp.transpose(table), index_rows, axis=0)
    return jnp.moveaxis(corner_rows, 2, 1)


def answer(reply):
    return lax.all_to_all(reply, ("mesh", "bg"), split_axis=0, concat_axis=0, tiled=True)


def assemble(local_part):
    padded_z = extended(local_part, (("mesh", 1),), 1)
    partial_sum = local_part.at[:, 0].add(padded_z[:, 0]).at[:, -1].add(padded_z[:, -1])
    padded_y = extended(partial_sum, (("bg", 2),), 1)
    summed = partial_sum.at[:, :, 0].add(padded_y[:, :, 0]).at[:, :, -1].add(padded_y[:, :, -1])
    return summed


def shards(displacement, bg_coef, query_elem, query_point, query_coord):
    devices = lax.axis_size("mesh") * lax.axis_size("bg")
    z_elems = displacement.shape[1] // 2
    y_elems = displacement.shape[2] // 2
    x_elems = displacement.shape[3] // 2
    tables = (
        basis_tables(z_elems, False) + basis_tables(y_elems, False) + basis_tables(x_elems, True)
    )
    weights = quad_weights(z_elems, y_elems, x_elems)
    point_count = 27 * z_elems * y_elems * x_elems
    elem_ids = query_elem.reshape(devices, 1, -1)
    coords = query_coord.reshape(devices, 3, -1)
    fetched = answer(
        gather_coefs(
            bg_coef,
            lax.all_to_all(elem_ids, ("mesh", "bg"), split_axis=0, concat_axis=0, tiled=True),
        )
    )
    found_vals = inverse_square(fetched, coords).reshape(-1)
    target_size_scale = (
        jnp.zeros((point_count,), jnp.float32)
        .at[query_point.reshape(-1)]
        .set(found_vals, mode="drop")
    )
    target_size_scale = target_size_scale.reshape(3 * z_elems, 3 * y_elems, 3 * x_elems)

    def local_energy(values):
        return energy(values, tables, target_size_scale, weights)

    node_field = assemble(jnp.pad(displacement, ((0, 0), (0, 1), (0, 1), (0, 0))))
    history = []
    for newton_pass in range(PASSES):
        direction = -assemble(jax.grad(local_energy)(node_field))
        partial_terms = jnp.stack(
            line_terms(node_field, direction, tables, target_size_scale, weights)
        )
        totals = lax.psum(partial_terms, ("mesh", "bg"))
        step_len = line_search(totals)
        node_field = node_field + step_len * direction
        history.append(totals[:5] / (devices * z_elems * y_elems * x_elems))
    return (node_field[:, :-1, :-1], jnp.stack(history))


def solution(mesh):
    in_specs = (
        P(None, "mesh", "bg", None),
        P(None, ("mesh", "bg")),
        P(("mesh", "bg"), None, None),
        P(("mesh", "bg"), None, None),
        P(("mesh", "bg"), None, None, None),
    )
    out_specs = (P(None, "mesh", "bg", None), P())
    return jax.shard_map(shards, mesh=mesh, in_specs=in_specs, out_specs=out_specs, check_vma=False)
```

profile of v0, /device:TPU:1, one launch (start us, length us, event | category | flops | bytes accessed | tf_op | source)
XLA Modules:
  0.0 415.2 jit_solution(10419066818697922350)
XLA Ops:
  0.7 2.1 collective-permute-start
  2.8 1.6 copy.164
  4.4 10.7 %all-to-all-start = ((s32[128,1,136]{2,1,0:T(1,128)}), s32[128,1,136]{2,1,0:T(1,128)S(1)}, u32[]{:S(2)}, u32[]{:S(2)}) async-start(s32[128,1,136]{2,1,0:T(1,128)} %bitcast.21), calls=%async_computation | async-start | bytes 262144 | tf_op jit(solution)/shard_map/all_to_all | solution.py:167
  15.1 1.0 copy.160
  16.9 1.0 fusion.53
  18.0 5.5 %collective-permute-start.1 = (f32[3,1,5,128]{3,1,2,0:T(1,128)S(1)}, f32[3,1,5,128]{3,1,2,0:T(1,128)S(1)}, u32[]{:S(2)}, u32[]{:S(2)}) collective-permute-start(f32[3,1,5,128]{3,1,2,0:T(1,128)S(1)} %get-tuple-element.209), channel_id=1, source_target_pairs={{8,0},{16,8},{24,16},{32,24},{40,32},{48,40},{56,48},{64,56},{72,6... | collective-permute-start | bytes 23048 | tf_op jit(solution)/shard_map/ppermute | solution.py:22
  24.3 2.4 collective-permute-start.2
  27.5 2.4 collective-permute-start.3
  29.9 5.3 %copy.167 = f32[8,16384]{0,1:T(8,128)} copy(f32[8,16384]{1,0:T(8,128)S(1)} %copy-done.4) | data formatting | bytes 1048576 | tf_op args[1]
  37.8 61.3 %gather_fusion = f32[17408,8]{1,0:T(8,128)} fusion(f32[16384,8]{1,0:T(8,128)} %bitcast.265, s32[17408]{0:T(1024)S(1)} %broadcast_clamp_fusion), kind=kCustom, calls=%fused_computation | custom fusion | bytes 1183744 | tf_op jit(solution)/shard_map/jit(_take)/gather | solution.py:136
  99.1 6.7 %copy.168 = f32[128,136,8]{1,2,0:T(8,128)S(1)} copy(f32[128,136,8]{2,1,0:T(8,128)} %bitcast.266) | data formatting | bytes 1114112 | tf_op jit(solution)/shard_map/jit(_take)/gather | solution.py:136
  106.1 1.1 select_bitcast_fusion
  107.2 7.9 %all-to-all-start.1 = ((f32[128,8,136]{2,1,0:T(8,128)}), f32[128,8,136]{2,1,0:T(8,128)S(1)}, u32[]{:S(2)}, u32[]{:S(2)}) async-start(f32[128,8,136]{2,1,0:T(8,128)} %select_bitcast_fusion), calls=%async_computation.1 | async-start | bytes 2097152 | tf_op jit(solution)/shard_map/all_to_all | solution.py:141
  116.3 17.6 %all-to-all-done.1 = f32[128,8,136]{2,1,0:T(8,128)S(1)} async-done(((f32[128,8,136]{2,1,0:T(8,128)}), f32[128,8,136]{2,1,0:T(8,128)S(1)}, u32[]{:S(2)}, u32[]{:S(2)}) %all-to-all-start.1) | async-done | bytes 557088 | tf_op jit(solution)/shard_map/all_to_all | solution.py:141
  133.9 2.9 slice_reduce_fusion.6
  137.9 64.3 %scatter_custom_fusion = f32[6912]{0:T(1024)S(1)} fusion(s32[17408]{0:T(1024)} %bitcast.268, f32[17408]{0:T(1024)S(1)} %multiply_exponential_fusion, f32[]{:T(128)} %constant.313.clone.1), kind=kCustom, calls=%fused_computation.166 | custom fusion | bytes 28160 | tf_op jit(solution)/shard_map/scatter | solution.py:174
  205.6 5.3 %collective-permute-done.4 = f32[3,1,5,128]{3,1,2,0:T(1,128)S(1)} collective-permute-done((f32[3,1,5,128]{3,1,2,0:T(1,128)S(1)}, f32[3,1,5,128]{3,1,2,0:T(1,128)S(1)}, u32[]{:S(2)}, u32[]{:S(2)}) %collective-permute-start.4) | collective-permute-done | bytes 7712 | tf_op jit(solution)/shard_map/ppermute | solution.py:19
  211.1 2.4 collective-permute-done.5
  213.7 3.6 collective-permute-start.6
  217.3 0.8 collective-permute-done.6
  218.1 3.5 collective-permute-start.7
  221.7 0.8 collective-permute-done.7
  228.9 2.0 stack.121
  230.9 65.5 %psum.14 = f32[6]{0:T(128)S(1)} all-reduce(f32[6]{0:T(128)S(1)} %stack.121), channel_id=1, replica_groups=mesh['mesh'=16,'bg'=8] {'mesh','bg'}, use_global_device_ids=true, to_apply=%region_18.19 | all-reduce | flops 6 | bytes 48 | tf_op jit(solution)/shard_map/psum | solution.py:188
  312.5 5.8 %collective-permute-done.8 = f32[3,1,5,128]{3,1,2,0:T(1,128)S(1)} collective-permute-done((f32[3,1,5,128]{3,1,2,0:T(1,128)S(1)}, f32[3,1,5,128]{3,1,2,0:T(1,128)S(1)}, u32[]{:S(2)}, u32[]{:S(2)}) %collective-permute-start.8) | collective-permute-done | bytes 7712 | tf_op jit(solution)/shard_map/ppermute | solution.py:19
  318.5 2.4 collective-permute-done.9
  321.0 1.8 collective-permute-start.10
  322.8 2.2 collective-permute-done.10
  325.1 3.7 collective-permute-start.11
  328.7 0.8 collective-permute-done.11
  336.0 2.0 stack.136
  338.0 65.3 %psum.15 = f32[6]{0:T(128)S(1)} all-reduce(f32[6]{0:T(128)S(1)} %stack.136), channel_id=1, replica_groups=mesh['mesh'=16,'bg'=8] {'mesh','bg'}, use_global_device_ids=true, to_apply=%region_36.37 | all-reduce | flops 6 | bytes 48 | tf_op jit(solution)/shard_map/psum | solution.py:188
  (149 shorter events, 26.8 us)
Async XLA Ops:
  0.6 22.8 %copy-start.7 = (f32[6]{0:T(128)S(1)}, f32[6]{0:T(128)}, u32[]{:S(2)}) copy-start(f32[6]{0:T(128)} %constant.334.clone) | copy-start | bytes 76
  0.6 26.0 %copy-start.6 = (f32[192]{0:T(256)S(1)}, f32[192]{0:T(256)}, u32[]{:S(2)}) copy-start(f32[192]{0:T(256)} %constant.335.clone) | copy-start | bytes 2308
  0.7 17.2 %copy-start.5 = (f32[3,4,4,128]{3,2,1,0:T(4,128)S(1)}, f32[3,4,4,128]{3,2,1,0:T(4,128)}, u32[]{:S(2)}) copy-start(f32[3,4,4,128]{3,2,1,0:T(4,128)} %param.38) | copy-start | bytes 73732
  0.7 29.2 %copy-start.4 = (f32[8,16384]{1,0:T(8,128)S(1)}, f32[8,16384]{1,0:T(8,128)}, u32[]{:S(2)}) copy-start(f32[8,16384]{1,0:T(8,128)} %param.39) | copy-start | bytes 1572868
  0.7 17.2 %collective-permute-start = (f32[3,1,5,128]{3,1,2,0:T(1,128)S(1)}, f32[3,1,5,128]{3,1,2,0:T(1,128)S(1)}, u32[]{:S(2)}, u32[]{:S(2)}) collective-permute-start(f32[3,1,5,128]{3,1,2,0:T(1,128)S(1)} %slice.391), channel_id=1, source_target_pairs={{0,8},{8,16},{16,24},{24,32},{32,40},{40,48},{48,56},{56,64},{64,7... | collective-permute-start | bytes 23048 | tf_op jit(solution)/shard_map/ppermute | solution.py:19
  4.4 32.8 %all-to-all-start = ((s32[128,1,136]{2,1,0:T(1,128)}), s32[128,1,136]{2,1,0:T(1,128)S(1)}, u32[]{:S(2)}, u32[]{:S(2)}) async-start(s32[128,1,136]{2,1,0:T(1,128)} %bitcast.21), calls=%async_computation | async-start | bytes 262144 | tf_op jit(solution)/shard_map/all_to_all | solution.py:167
  18.0 6.2 %collective-permute-start.1 = (f32[3,1,5,128]{3,1,2,0:T(1,128)S(1)}, f32[3,1,5,128]{3,1,2,0:T(1,128)S(1)}, u32[]{:S(2)}, u32[]{:S(2)}) collective-permute-start(f32[3,1,5,128]{3,1,2,0:T(1,128)S(1)} %get-tuple-element.209), channel_id=1, source_target_pairs={{8,0},{16,8},{24,16},{32,24},{40,32},{48,40},{56,48},{64,56},{72,6... | collective-permute-start | bytes 23048 | tf_op jit(solution)/shard_map/ppermute | solution.py:22
  24.3 3.2 collective-permute-start.2
  27.5 8.3 %collective-permute-start.3 = (f32[3,5,1,128]{3,1,2,0:T(8,128)S(1)}, f32[3,5,1,128]{3,1,2,0:T(8,128)S(1)}, u32[]{:S(2)}, u32[]{:S(2)}) collective-permute-start(f32[3,5,1,128]{3,1,2,0:T(8,128)S(1)} %get-tuple-element.207), channel_id=1, source_target_pairs={{1,0},{2,1},{3,2},{4,3},{5,4},{6,5},{7,6},{0,7},{9,8},{10,9},{11,1... | collective-permute-start | bytes 23048 | tf_op jit(solution)/shard_map/ppermute | solution.py:22
  29.9 6.0 %copy-start.3 = (f32[5,6,1,1]{0,1,3,2:T(8,128)S(1)}, f32[5,6,1,1]{0,1,3,2:T(8,128)}, u32[]{:S(2)}) copy-start(f32[5,6,1,1]{0,1,3,2:T(8,128)} %constant.344) | copy-start | bytes 364
  35.2 0.9 copy-start.2
  35.2 1.7 copy-start
  107.2 8.3 %copy-start.1 = (f32[128,192,1,1]{0,1,3,2:T(8,128)S(1)}, f32[128,192,1,1]{0,1,3,2:T(8,128)}, u32[]{:S(2)}) copy-start(f32[128,192,1,1]{0,1,3,2:T(8,128)} %constant.343) | copy-start | bytes 294916
  107.2 26.7 %all-to-all-start.1 = ((f32[128,8,136]{2,1,0:T(8,128)}), f32[128,8,136]{2,1,0:T(8,128)S(1)}, u32[]{:S(2)}, u32[]{:S(2)}) async-start(f32[128,8,136]{2,1,0:T(8,128)} %select_bitcast_fusion), calls=%async_computation.1 | async-start | bytes 2097152 | tf_op jit(solution)/shard_map/all_to_all | solution.py:141
  205.1 5.9 %collective-permute-start.4 = (f32[3,1,5,128]{3,1,2,0:T(1,128)S(1)}, f32[3,1,5,128]{3,1,2,0:T(1,128)S(1)}, u32[]{:S(2)}, u32[]{:S(2)}) collective-permute-start(f32[3,1,5,128]{3,1,2,0:T(1,128)S(1)} %slice.440), channel_id=1, source_target_pairs={{0,8},{8,16},{16,24},{24,32},{32,40},{40,48},{48,56},{56,64},{64,7... | collective-permute-start | bytes 23048 | tf_op jit(solution)/shard_map/ppermute | solution.py:19
  211.0 2.6 collective-permute-start.5
  213.7 4.5 %collective-permute-start.6 = (f32[3,5,1,128]{3,1,2,0:T(8,128)S(1)}, f32[3,5,1,128]{3,1,2,0:T(8,128)S(1)}, u32[]{:S(2)}, u32[]{:S(2)}) collective-permute-start(f32[3,5,1,128]{3,1,2,0:T(8,128)S(1)} %slice.443), channel_id=1, source_target_pairs={{0,1},{1,2},{2,3},{3,4},{4,5},{5,6},{6,7},{7,0},{8,9},{9,10},{10,1... | collective-permute-start | bytes 23048 | tf_op jit(solution)/shard_map/ppermute | solution.py:19
  218.1 4.3 %collective-permute-start.7 = (f32[3,5,1,128]{3,1,2,0:T(8,128)S(1)}, f32[3,5,1,128]{3,1,2,0:T(8,128)S(1)}, u32[]{:S(2)}, u32[]{:S(2)}) collective-permute-start(f32[3,5,1,128]{3,1,2,0:T(8,128)S(1)} %get-tuple-element.203), channel_id=1, source_target_pairs={{1,0},{2,1},{3,2},{4,3},{5,4},{6,5},{7,6},{0,7},{9,8},{10,9},{11,1... | collective-permute-start | bytes 23048 | tf_op jit(solution)/shard_map/ppermute | solution.py:22
  312.4 5.9 %collective-permute-start.8 = (f32[3,1,5,128]{3,1,2,0:T(1,128)S(1)}, f32[3,1,5,128]{3,1,2,0:T(1,128)S(1)}, u32[]{:S(2)}, u32[]{:S(2)}) collective-permute-start(f32[3,1,5,128]{3,1,2,0:T(1,128)S(1)} %slice.446), channel_id=1, source_target_pairs={{0,8},{8,16},{16,24},{24,32},{32,40},{40,48},{48,56},{56,64},{64,7... | collective-permute-start | bytes 23048 | tf_op jit(solution)/shard_map/ppermute | solution.py:19
  318.3 2.6 collective-permute-start.9
  321.0 4.1 collective-permute-start.10
  325.1 4.5 %collective-permute-start.11 = (f32[3,5,1,128]{3,1,2,0:T(8,128)S(1)}, f32[3,5,1,128]{3,1,2,0:T(8,128)S(1)}, u32[]{:S(2)}, u32[]{:S(2)}) collective-permute-start(f32[3,5,1,128]{3,1,2,0:T(8,128)S(1)} %get-tuple-element.199), channel_id=1, source_target_pairs={{1,0},{2,1},{3,2},{4,3},{5,4},{6,5},{7,6},{0,7},{9,8},{10,9},{11,1... | collective-permute-start | bytes 23048 | tf_op jit(solution)/shard_map/ppermute | solution.py:22
where the time goes:
time: 416 us; the launch traced here: 415 us
  local copies, waits for them, and re-layouts  153 us (37%)
  blocking collectives  131 us (31%)
  starting transfers between devices  44.3 us (11%)
  waiting for transfers between devices  39.7 us (10%)
  between operations  26.7 us (6%)
  matrix products  12.1 us (3%)
  other arithmetic  9.06 us (2%)
    psum x2, blocking collectives, shards(): totals = lax.psum(partial_terms, ('mesh', 'bg'))  131 us
    gather x2, local copies, waits for them, and re-layouts, gather_coefs(): corner_rows = jnp.take(jnp.transpose(table), index_rows, axis=0)  68 us
    scatter x1, local copies, waits for them, and re-layouts, shards(): target_size_scale = jnp.zeros((point_count,), jnp.float32).at[query_point...  64.3 us
    all_to_all x1, waiting for transfers between devices, answer(): lax.all_to_all(reply, ('mesh', 'bg'), split_axis=0, concat_axis=0, tiled=...  17.6 us
    ppermute x6, starting transfers between devices, extended(): lax.ppermute(lax.slice_in_dim(block, 0, width, axis=dim), axis, backward)  15.1 us
    ppermute x6, waiting for transfers between devices, extended(): lax.ppermute(lax.slice_in_dim(block, block.shape[dim] - width, None, axis...  15 us
    all_to_all x1, starting transfers between devices, shards(): lax.all_to_all(elem_ids, ('mesh', 'bg'), split_axis=0, concat_axis=0, til...  10.7 us
    ppermute x6, starting transfers between devices, extended(): lax.ppermute(lax.slice_in_dim(block, block.shape[dim] - width, None, axis...  10.6 us
  transfers between devices with their start and end apart: 14, of which 11 were waited for; matrix products, arithmetic and copies ran while one was open for 3% of the time, Pallas kernels for 0%

commit v1 on v0

--- a/solution.py
+++ b/solution.py
@@ -1,13 +1,24 @@
+import functools
 import jax
 import jax.numpy as jnp
 import numpy as np
 from jax import lax
 from jax.sharding import PartitionSpec as P
+from jax.lax import psum
 
 PASSES = 2
 LS_STEPS = 4
 GAUSS_POINTS = np.array([0.5 - 0.5 * np.sqrt(0.6), 0.5, 0.5 + 0.5 * np.sqrt(0.6)])
 GAUSS_WEIGHTS = np.array([5.0 / 18.0, 8.0 / 18.0, 5.0 / 18.0])
+
+
+def edges_obtain(block_here, shard_axis, chip_axis):
+    for dev_j in (shard_axis, chip_axis):
+        block_here = psum(block_here, dev_j)
+    return block_here
+
+
+goods_cover = functools.partial(edges_obtain, shard_axis="bg", chip_axis="mesh")
 
 
 def extended(block, sides, width):
@@ -185,7 +196,7 @@
         partial_terms = jnp.stack(
             line_terms(node_field, direction, tables, target_size_scale, weights)
         )
-        totals = lax.psum(partial_terms, ("mesh", "bg"))
+        totals = goods_cover(partial_terms)
         step_len = line_search(totals)
         node_field = node_field + step_len * direction
         history.append(totals[:5] / (devices * z_elems * y_elems * x_elems))

time: 416 us -> 392 us (0.942)
  the two profiles are of different devices: /device:TPU:1 before, /device:TPU:0 now
where the time goes in v1:
time: 392 us; the launch traced here: 391 us
  local copies, waits for them, and re-layouts  153 us (39%)
  blocking collectives  108 us (28%)
  waiting for transfers between devices  55 us (14%)
  starting transfers between devices  27.7 us (7%)
  between operations  26.7 us (7%)
  matrix products  12.1 us (3%)
  other arithmetic  9.06 us (2%)
    psum x4, blocking collectives, edges_obtain(): block_here = psum(block_here, dev_j)  108 us
    gather x2, local copies, waits for them, and re-layouts, gather_coefs(): corner_rows = jnp.take(jnp.transpose(table), index_rows, axis=0)  68 us
    scatter x1, local copies, waits for them, and re-layouts, shards(): target_size_scale = jnp.zeros((point_count,), jnp.float32).at[query_point...  64.3 us
    ppermute x6, waiting for transfers between devices, extended(): lax.ppermute(lax.slice_in_dim(block, block.shape[dim] - width, None, axis...  26.1 us
    all_to_all x1, waiting for transfers between devices, answer(): lax.all_to_all(reply, ('mesh', 'bg'), split_axis=0, concat_axis=0, tiled=...  17.7 us
    ppermute x6, waiting for transfers between devices, extended(): lax.ppermute(lax.slice_in_dim(block, 0, width, axis=dim), axis, backward)  11.2 us
    all_to_all x1, starting transfers between devices, shards(): lax.all_to_all(elem_ids, ('mesh', 'bg'), split_axis=0, concat_axis=0, til...  10.8 us
    all_to_all x1, starting transfers between devices, answer(): lax.all_to_all(reply, ('mesh', 'bg'), split_axis=0, concat_axis=0, tiled=...  9.14 us
  transfers between devices with their start and end apart: 14, of which 11 were waited for; matrix products, arithmetic and copies ran while one was open for 3% of the time, Pallas kernels for 0%

profile of v1, /device:TPU:0, one launch (start us, length us, event | category | flops | bytes accessed | tf_op | source)
XLA Modules:
  0.0 391.4 jit_solution(6061046410397599413)
XLA Ops:
  0.7 1.7 collective-permute-start
  2.4 1.6 copy.164
  4.0 10.8 %all-to-all-start = ((s32[128,1,136]{2,1,0:T(1,128)}), s32[128,1,136]{2,1,0:T(1,128)S(1)}, u32[]{:S(2)}, u32[]{:S(2)}) async-start(s32[128,1,136]{2,1,0:T(1,128)} %bitcast.21), calls=%async_computation | async-start | bytes 262144 | tf_op jit(solution)/shard_map/all_to_all | solution.py:178
  14.8 1.0 copy.160
  16.6 1.0 fusion.53
  17.6 5.1 %collective-permute-start.1 = (f32[3,1,5,128]{3,1,2,0:T(1,128)S(1)}, f32[3,1,5,128]{3,1,2,0:T(1,128)S(1)}, u32[]{:S(2)}, u32[]{:S(2)}) collective-permute-start(f32[3,1,5,128]{3,1,2,0:T(1,128)S(1)} %get-tuple-element.209), channel_id=1, source_target_pairs={{8,0},{16,8},{24,16},{32,24},{40,32},{48,40},{56,48},{64,56},{72,6... | collective-permute-start | bytes 23048 | tf_op jit(solution)/shard_map/ppermute | solution.py:33
  22.8 1.2 collective-permute-done.1
  24.3 4.2 %collective-permute-done.2 = f32[3,5,1,128]{3,1,2,0:T(8,128)S(1)} collective-permute-done((f32[3,5,1,128]{3,1,2,0:T(8,128)S(1)}, f32[3,5,1,128]{3,1,2,0:T(8,128)S(1)}, u32[]{:S(2)}, u32[]{:S(2)}) %collective-permute-start.2) | collective-permute-done | bytes 7712 | tf_op jit(solution)/shard_map/ppermute | solution.py:30
  28.5 5.3 %copy.167 = f32[8,16384]{0,1:T(8,128)} copy(f32[8,16384]{1,0:T(8,128)S(1)} %copy-done.4) | data formatting | bytes 1048576 | tf_op args[1]
  36.5 61.3 %gather_fusion = f32[17408,8]{1,0:T(8,128)} fusion(f32[16384,8]{1,0:T(8,128)} %bitcast.265, s32[17408]{0:T(1024)S(1)} %broadcast_clamp_fusion), kind=kCustom, calls=%fused_computation | custom fusion | bytes 1183744 | tf_op jit(solution)/shard_map/jit(_take)/gather | solution.py:147
  97.7 6.7 %copy.168 = f32[128,136,8]{1,2,0:T(8,128)S(1)} copy(f32[128,136,8]{2,1,0:T(8,128)} %bitcast.266) | data formatting | bytes 1114112 | tf_op jit(solution)/shard_map/jit(_take)/gather | solution.py:147
  104.7 1.1 select_bitcast_fusion
  105.9 9.1 %all-to-all-start.1 = ((f32[128,8,136]{2,1,0:T(8,128)}), f32[128,8,136]{2,1,0:T(8,128)S(1)}, u32[]{:S(2)}, u32[]{:S(2)}) async-start(f32[128,8,136]{2,1,0:T(8,128)} %select_bitcast_fusion), calls=%async_computation.1 | async-start | bytes 2097152 | tf_op jit(solution)/shard_map/all_to_all | solution.py:152
  116.2 17.7 %all-to-all-done.1 = f32[128,8,136]{2,1,0:T(8,128)S(1)} async-done(((f32[128,8,136]{2,1,0:T(8,128)}), f32[128,8,136]{2,1,0:T(8,128)S(1)}, u32[]{:S(2)}, u32[]{:S(2)}) %all-to-all-start.1) | async-done | bytes 557088 | tf_op jit(solution)/shard_map/all_to_all | solution.py:152
  133.9 2.9 slice_reduce_fusion.6
  137.9 64.3 %scatter_custom_fusion = f32[6912]{0:T(1024)S(1)} fusion(s32[17408]{0:T(1024)} %bitcast.268, f32[17408]{0:T(1024)S(1)} %multiply_exponential_fusion, f32[]{:T(128)} %constant.313.clone.1), kind=kCustom, calls=%fused_computation.166 | custom fusion | bytes 28160 | tf_op jit(solution)/shard_map/scatter | solution.py:185
  205.8 6.3 %collective-permute-done.4 = f32[3,1,5,128]{3,1,2,0:T(1,128)S(1)} collective-permute-done((f32[3,1,5,128]{3,1,2,0:T(1,128)S(1)}, f32[3,1,5,128]{3,1,2,0:T(1,128)S(1)}, u32[]{:S(2)}, u32[]{:S(2)}) %collective-permute-start.4) | collective-permute-done | bytes 7712 | tf_op jit(solution)/shard_map/ppermute | solution.py:30
  212.3 3.6 collective-permute-done.5
  215.9 4.3 %collective-permute-done.6 = f32[3,5,1,128]{3,1,2,0:T(8,128)S(1)} collective-permute-done((f32[3,5,1,128]{3,1,2,0:T(8,128)S(1)}, f32[3,5,1,128]{3,1,2,0:T(8,128)S(1)}, u32[]{:S(2)}, u32[]{:S(2)}) %collective-permute-start.6) | collective-permute-done | bytes 7712 | tf_op jit(solution)/shard_map/ppermute | solution.py:30
  220.3 1.4 collective-permute-done.7
  224.8 0.8 fusion.37
  228.1 2.0 stack.121
  230.1 15.3 %psum.28 = f32[6]{0:T(128)S(1)} all-reduce(f32[6]{0:T(128)S(1)} %stack.121), channel_id=1, replica_groups=mesh['mesh'=16,'bg'=8] {'bg'}, use_global_device_ids=true, to_apply=%region_18.19 | all-reduce | flops 6 | bytes 48 | tf_op jit(solution)/shard_map/psum | solution.py:17
  245.4 39.0 %psum.29 = f32[6]{0:T(128)S(1)} all-reduce(f32[6]{0:T(128)S(1)} %psum.28), channel_id=1, replica_groups=mesh['mesh'=16,'bg'=8] {'mesh'}, use_global_device_ids=true, to_apply=%region_19.20 | all-reduce | flops 6 | bytes 48 | tf_op jit(solution)/shard_map/psum | solution.py:17
  300.5 7.0 %collective-permute-done.8 = f32[3,1,5,128]{3,1,2,0:T(1,128)S(1)} collective-permute-done((f32[3,1,5,128]{3,1,2,0:T(1,128)S(1)}, f32[3,1,5,128]{3,1,2,0:T(1,128)S(1)}, u32[]{:S(2)}, u32[]{:S(2)}) %collective-permute-start.8) | collective-permute-done | bytes 7712 | tf_op jit(solution)/shard_map/ppermute | solution.py:30
  307.6 3.6 collective-permute-done.9
  311.3 4.3 %collective-permute-done.10 = f32[3,5,1,128]{3,1,2,0:T(8,128)S(1)} collective-permute-done((f32[3,5,1,128]{3,1,2,0:T(8,128)S(1)}, f32[3,5,1,128]{3,1,2,0:T(8,128)S(1)}, u32[]{:S(2)}, u32[]{:S(2)}) %collective-permute-start.10) | collective-permute-done | bytes 7712 | tf_op jit(solution)/shard_map/ppermute | solution.py:30
  315.6 1.4 collective-permute-done.11
  320.1 0.8 fusion.43
  323.5 2.0 stack.136
  325.5 15.3 %psum.30 = f32[6]{0:T(128)S(1)} all-reduce(f32[6]{0:T(128)S(1)} %stack.136), channel_id=1, replica_groups=mesh['mesh'=16,'bg'=8] {'bg'}, use_global_device_ids=true, to_apply=%region_37.38 | all-reduce | flops 6 | bytes 48 | tf_op jit(solution)/shard_map/psum | solution.py:17
  340.8 38.8 %psum.31 = f32[6]{0:T(128)S(1)} all-reduce(f32[6]{0:T(128)S(1)} %psum.30), channel_id=1, replica_groups=mesh['mesh'=16,'bg'=8] {'mesh'}, use_global_device_ids=true, to_apply=%region_38.39 | all-reduce | flops 6 | bytes 48 | tf_op jit(solution)/shard_map/psum | solution.py:17
  (151 shorter events, 24.0 us)
Async XLA Ops:
  0.6 22.1 %copy-start.7 = (f32[6]{0:T(128)S(1)}, f32[6]{0:T(128)}, u32[]{:S(2)}) copy-start(f32[6]{0:T(128)} %constant.334.clone) | copy-start | bytes 76
  0.6 23.5 %copy-start.6 = (f32[192]{0:T(256)S(1)}, f32[192]{0:T(256)}, u32[]{:S(2)}) copy-start(f32[192]{0:T(256)} %constant.335.clone) | copy-start | bytes 2308
  0.7 16.9 %copy-start.5 = (f32[3,4,4,128]{3,2,1,0:T(4,128)S(1)}, f32[3,4,4,128]{3,2,1,0:T(4,128)}, u32[]{:S(2)}) copy-start(f32[3,4,4,128]{3,2,1,0:T(4,128)} %param.38) | copy-start | bytes 73732
  0.7 27.8 %copy-start.4 = (f32[8,16384]{1,0:T(8,128)S(1)}, f32[8,16384]{1,0:T(8,128)}, u32[]{:S(2)}) copy-start(f32[8,16384]{1,0:T(8,128)} %param.39) | copy-start | bytes 1572868
  0.7 16.9 %collective-permute-start = (f32[3,1,5,128]{3,1,2,0:T(1,128)S(1)}, f32[3,1,5,128]{3,1,2,0:T(1,128)S(1)}, u32[]{:S(2)}, u32[]{:S(2)}) collective-permute-start(f32[3,1,5,128]{3,1,2,0:T(1,128)S(1)} %slice.391), channel_id=1, source_target_pairs={{0,8},{8,16},{16,24},{24,32},{32,40},{40,48},{48,56},{56,64},{64,7... | collective-permute-start | bytes 23048 | tf_op jit(solution)/shard_map/ppermute | solution.py:30
  4.0 31.9 %all-to-all-start = ((s32[128,1,136]{2,1,0:T(1,128)}), s32[128,1,136]{2,1,0:T(1,128)S(1)}, u32[]{:S(2)}, u32[]{:S(2)}) async-start(s32[128,1,136]{2,1,0:T(1,128)} %bitcast.21), calls=%async_computation | async-start | bytes 262144 | tf_op jit(solution)/shard_map/all_to_all | solution.py:178
  17.6 6.4 %collective-permute-start.1 = (f32[3,1,5,128]{3,1,2,0:T(1,128)S(1)}, f32[3,1,5,128]{3,1,2,0:T(1,128)S(1)}, u32[]{:S(2)}, u32[]{:S(2)}) collective-permute-start(f32[3,1,5,128]{3,1,2,0:T(1,128)S(1)} %get-tuple-element.209), channel_id=1, source_target_pairs={{8,0},{16,8},{24,16},{32,24},{40,32},{48,40},{56,48},{64,56},{72,6... | collective-permute-start | bytes 23048 | tf_op jit(solution)/shard_map/ppermute | solution.py:33
  24.2 4.3 %collective-permute-start.2 = (f32[3,5,1,128]{3,1,2,0:T(8,128)S(1)}, f32[3,5,1,128]{3,1,2,0:T(8,128)S(1)}, u32[]{:S(2)}, u32[]{:S(2)}) collective-permute-start(f32[3,5,1,128]{3,1,2,0:T(8,128)S(1)} %slice.426), channel_id=1, source_target_pairs={{0,1},{1,2},{2,3},{3,4},{4,5},{5,6},{6,7},{7,0},{8,9},{9,10},{10,1... | collective-permute-start | bytes 23048 | tf_op jit(solution)/shard_map/ppermute | solution.py:30
  28.5 6.0 %collective-permute-start.3 = (f32[3,5,1,128]{3,1,2,0:T(8,128)S(1)}, f32[3,5,1,128]{3,1,2,0:T(8,128)S(1)}, u32[]{:S(2)}, u32[]{:S(2)}) collective-permute-start(f32[3,5,1,128]{3,1,2,0:T(8,128)S(1)} %get-tuple-element.207), channel_id=1, source_target_pairs={{1,0},{2,1},{3,2},{4,3},{5,4},{6,5},{7,6},{0,7},{9,8},{10,9},{11,1... | collective-permute-start | bytes 23048 | tf_op jit(solution)/shard_map/ppermute | solution.py:33
  28.5 6.0 %copy-start.3 = (f32[5,6,1,1]{0,1,3,2:T(8,128)S(1)}, f32[5,6,1,1]{0,1,3,2:T(8,128)}, u32[]{:S(2)}) copy-start(f32[5,6,1,1]{0,1,3,2:T(8,128)} %constant.344) | copy-start | bytes 364
  33.8 0.9 copy-start.2
  33.8 1.7 copy-start
  105.9 9.5 %copy-start.1 = (f32[128,192,1,1]{0,1,3,2:T(8,128)S(1)}, f32[128,192,1,1]{0,1,3,2:T(8,128)}, u32[]{:S(2)}) copy-start(f32[128,192,1,1]{0,1,3,2:T(8,128)} %constant.343) | copy-start | bytes 294916
  105.9 28.0 %all-to-all-start.1 = ((f32[128,8,136]{2,1,0:T(8,128)}), f32[128,8,136]{2,1,0:T(8,128)S(1)}, u32[]{:S(2)}, u32[]{:S(2)}) async-start(f32[128,8,136]{2,1,0:T(8,128)} %select_bitcast_fusion), calls=%async_computation.1 | async-start | bytes 2097152 | tf_op jit(solution)/shard_map/all_to_all | solution.py:152
  205.1 7.0 %collective-permute-start.4 = (f32[3,1,5,128]{3,1,2,0:T(1,128)S(1)}, f32[3,1,5,128]{3,1,2,0:T(1,128)S(1)}, u32[]{:S(2)}, u32[]{:S(2)}) collective-permute-start(f32[3,1,5,128]{3,1,2,0:T(1,128)S(1)} %slice.440), channel_id=1, source_target_pairs={{0,8},{8,16},{16,24},{24,32},{32,40},{40,48},{48,56},{56,64},{64,7... | collective-permute-start | bytes 23048 | tf_op jit(solution)/shard_map/ppermute | solution.py:30
  212.1 3.7 collective-permute-start.5
  215.9 4.3 %collective-permute-start.6 = (f32[3,5,1,128]{3,1,2,0:T(8,128)S(1)}, f32[3,5,1,128]{3,1,2,0:T(8,128)S(1)}, u32[]{:S(2)}, u32[]{:S(2)}) collective-permute-start(f32[3,5,1,128]{3,1,2,0:T(8,128)S(1)} %slice.443), channel_id=1, source_target_pairs={{0,1},{1,2},{2,3},{3,4},{4,5},{5,6},{6,7},{7,0},{8,9},{9,10},{10,1... | collective-permute-start | bytes 23048 | tf_op jit(solution)/shard_map/ppermute | solution.py:30
  220.3 1.4 collective-permute-start.7
  300.4 7.0 %collective-permute-start.8 = (f32[3,1,5,128]{3,1,2,0:T(1,128)S(1)}, f32[3,1,5,128]{3,1,2,0:T(1,128)S(1)}, u32[]{:S(2)}, u32[]{:S(2)}) collective-permute-start(f32[3,1,5,128]{3,1,2,0:T(1,128)S(1)} %slice.446), channel_id=1, source_target_pairs={{0,8},{8,16},{16,24},{24,32},{32,40},{40,48},{48,56},{56,64},{64,7... | collective-permute-start | bytes 23048 | tf_op jit(solution)/shard_map/ppermute | solution.py:30
  307.5 3.7 collective-permute-start.9
  311.3 4.3 %collective-permute-start.10 = (f32[3,5,1,128]{3,1,2,0:T(8,128)S(1)}, f32[3,5,1,128]{3,1,2,0:T(8,128)S(1)}, u32[]{:S(2)}, u32[]{:S(2)}) collective-permute-start(f32[3,5,1,128]{3,1,2,0:T(8,128)S(1)} %slice.449), channel_id=1, source_target_pairs={{0,1},{1,2},{2,3},{3,4},{4,5},{5,6},{6,7},{7,0},{8,9},{9,10},{10,1... | collective-permute-start | bytes 23048 | tf_op jit(solution)/shard_map/ppermute | solution.py:30
  315.6 1.4 collective-permute-start.11
